TPU v7x, 128 devices: a whole 4x4x4 slice. The times are simulated.
128 devices in a mesh: row: 8 (over y, x_lo), col: 16 (over z, x_hi, core).
Axes of the slice: x: 4 (x_hi: 2, x_lo: 2; x = x_hi * 2 + x_lo), y: 4, z: 4, core: 2. Of those that a mesh axis runs over, the one named last changes fastest.
Arguments:
- pair: bfloat16 [256, 256, 128], P('row', 'col'), may hold values from -6 to 6
- cotangent: bfloat16 [256, 256, 128], P('row', 'col'), may hold values from -6 to 6
- token_mask: int32 [256], replicated, may hold values 0 or 1
- out_in_proj: bfloat16 [128, 640], replicated, may hold values from -0.5 to 0.5
- out_out_proj: bfloat16 [128, 128], replicated, may hold values from -0.5 to 0.5
- in_in_proj: bfloat16 [128, 640], replicated, may hold values from -0.5 to 0.5
- in_out_proj: bfloat16 [128, 128], replicated, may hold values from -0.5 to 0.5
Outputs:
- updated_pair: bfloat16 [256, 256, 128], P('row', 'col')
- pair_grad: bfloat16 [256, 256, 128], P('row', 'col')
- out_in_grad: float32 [128, 640], replicated
- out_out_grad: float32 [128, 128], replicated
- in_in_grad: float32 [128, 640], replicated
- in_out_grad: float32 [128, 128], replicated
All inputs are finite; a program needn't handle non-finite values.
Results may differ from a plain program's by a relative error of at most 0.012.
Values may be sent and summed in bfloat16 or wider, within the bound.
A program may use at most 128 MiB of HBM per device.

v0:
```python
import jax
import jax.numpy as jnp
from jax import lax
from jax.sharding import PartitionSpec as P

H = 128
EPSILON = 1e-05


def shortened(array):
    return jax.tree.map(lambda a: a.astype(jnp.bfloat16) if a.dtype == jnp.float32 else a, array)


def from_everyone(array, axis):
    copies = jnp.broadcast_to(array, (lax.axis_size(axis), *array.shape))
    return lax.all_to_all(copies, axis, split_axis=0, concat_axis=0, tiled=True)


def in_order(tiles, dim):
    shape = list(tiles.shape[1:])
    shape[dim] *= tiles.shape[0]
    return jnp.moveaxis(tiles, 0, dim).reshape(shape)


def collect(array, axis, dim):
    tiles = from_everyone(array, axis)
    return in_order(tiles, dim)


def normalize(values):
    centre = jnp.mean(values, axis=-1, keepdims=True)
    shifted = values - centre
    spread = jnp.mean(shifted * shifted, axis=-1, keepdims=True)
    return shifted * lax.rsqrt(spread + EPSILON)


def gating(projected, pair_mask):
    left_value = projected[..., :H]
    left_gate = projected[..., H : 2 * H]
    right_value = projected[..., 2 * H : 3 * H]
    right_gate = projected[..., 3 * H : 4 * H]
    left_full = jax.nn.sigmoid(left_gate) * left_value * pair_mask
    right_full = jax.nn.sigmoid(right_gate) * right_value * pair_mask
    return (left_full, right_full, jax.nn.sigmoid(projected[..., 4 * H :]))


def cols_of(tiles):
    return jax.tree.map(
        lambda part, own: part.astype(own.dtype),
        lax.all_gather(shortened(tiles), "col", axis=1, tiled=True),
        tiles,
    )


def rows_of(tiles):
    return jax.tree.map(
        lambda part, own: part.astype(own.dtype),
        jax.tree.map(lambda part: collect(part, "row", 0), shortened(tiles)),
        tiles,
    )


def to_row_blocks(panel):
    return lax.all_to_all(panel, "col", split_axis=0, concat_axis=1, tiled=True)


def to_col_blocks(panel):
    return lax.all_to_all(panel, "row", split_axis=1, concat_axis=0, tiled=True)


def outgoing_sum(left_tile, right_tile):
    row_panels = rows_of((left_tile, right_tile))
    left_panel = cols_of(left_tile)
    right_rows = to_row_blocks(row_panels[1])
    total = jnp.einsum("ikh,jkh->ijh", left_panel, right_rows, preferred_element_type=jnp.float32)
    return (total, row_panels)


def incoming_sum(left_tile, right_tile):
    col_panels = cols_of((left_tile, right_tile))
    right_all = rows_of(right_tile)
    left_cols = to_col_blocks(col_panels[0])
    total = jnp.einsum("kih,kjh->ijh", left_cols, right_all, preferred_element_type=jnp.float32)
    return (total, col_panels)


def outgoing_grads(tri_grad, row_panels):
    grad_cols = cols_of(tri_grad)
    grad_rows = to_col_blocks(grad_cols)
    left_grad = jnp.einsum(
        "ijh,jkh->ikh", grad_cols, row_panels[1], preferred_element_type=jnp.float32
    )
    right_grad = jnp.einsum(
        "ijh,ikh->jkh", grad_rows, row_panels[0], preferred_element_type=jnp.float32
    )
    return (left_grad, right_grad)


def incoming_grads(tri_grad, col_panels):
    grad_rows = rows_of(tri_grad)
    grad_cols = to_row_blocks(grad_rows)
    left_grad = jnp.einsum(
        "ijh,kjh->kih", grad_cols, col_panels[1], preferred_element_type=jnp.float32
    )
    right_grad = jnp.einsum(
        "kih,ijh->kjh", col_panels[0], grad_rows, preferred_element_type=jnp.float32
    )
    return (left_grad, right_grad)


def forward(pair_in, pair_mask, w_in, w_out, outgoing):
    pair_wide = pair_in.astype(jnp.float32)
    normed = normalize(pair_wide).astype(jnp.bfloat16)
    projected = jnp.dot(normed, w_in, preferred_element_type=jnp.float32)
    left_full, right_full, gate = gating(projected, pair_mask)
    left_tile = left_full.astype(jnp.bfloat16)
    right_tile = right_full.astype(jnp.bfloat16)
    if outgoing:
        triangle_sum, panels = outgoing_sum(left_tile, right_tile)
    else:
        triangle_sum, panels = incoming_sum(left_tile, right_tile)
    tri_normed = normalize(triangle_sum).astype(jnp.bfloat16)
    lifted = jnp.dot(tri_normed, w_out, preferred_element_type=jnp.float32)
    result = (pair_wide + gate * lifted).astype(jnp.bfloat16)
    saved = (pair_wide, normed, projected, gate, triangle_sum, tri_normed, lifted, panels)
    return (result, saved)


def backward(cotan, saved, pair_mask, w_in, w_out, outgoing):
    pair_wide, normed, projected, gate, triangle_sum, tri_normed, lifted, panels = saved
    cot_wide = cotan.astype(jnp.float32)
    lift_grad = gate * cot_wide
    gate_grad = lifted * cot_wide
    out_grad = jnp.einsum(
        "ijh,ijc->hc", tri_normed.astype(jnp.float32), lift_grad, precision=lax.Precision.HIGHEST
    )
    normed_tri_grad = jnp.dot(
        lift_grad, w_out.astype(jnp.float32).T, precision=lax.Precision.HIGHEST
    )
    tri_grad = jax.vjp(normalize, triangle_sum)[1](normed_tri_grad)[0].astype(jnp.bfloat16)
    if outgoing:
        left_grad, right_grad = outgoing_grads(tri_grad, panels)
    else:
        left_grad, right_grad = incoming_grads(tri_grad, panels)
    gate_vjp = jax.vjp(lambda values: gating(values, pair_mask), projected)[1]
    proj_grad = gate_vjp((left_grad, right_grad, gate_grad))[0]
    in_grad = jnp.einsum(
        "ijc,ijq->cq", normed.astype(jnp.float32), proj_grad, precision=lax.Precision.HIGHEST
    )
    normed_grad = jnp.dot(proj_grad, w_in.astype(jnp.float32).T, precision=lax.Precision.HIGHEST)
    pair_grad = (cot_wide + jax.vjp(normalize, pair_wide)[1](normed_grad)[0]).astype(jnp.bfloat16)
    return (pair_grad, in_grad, out_grad)


def local(pair, cotangent, token_mask, out_in_proj, out_out_proj, in_in_proj, in_out_proj):
    row_tile = pair.shape[0]
    col_tile = pair.shape[1]
    row_flags = lax.dynamic_slice_in_dim(
        token_mask, lax.axis_index("row") * row_tile, row_tile, 0
    ).astype(jnp.float32)
    col_flags = lax.dynamic_slice_in_dim(
        token_mask, lax.axis_index("col") * col_tile, col_tile, 0
    ).astype(jnp.float32)
    pair_mask = (row_flags[:, None] * col_flags[None, :])[:, :, None]
    middle, saved_out = forward(pair, pair_mask, out_in_proj, out_out_proj, True)
    updated, saved_in = forward(middle, pair_mask, in_in_proj, in_out_proj, False)
    middle_grad, in_in_part, in_out_part = backward(
        cotangent, saved_in, pair_mask, in_in_proj, in_out_proj, False
    )
    pair_grad, out_in_part, out_out_part = backward(
        middle_grad, saved_out, pair_mask, out_in_proj, out_out_proj, True
    )
    totals = lax.psum((out_in_part, out_out_part, in_in_part, in_out_part), ("row", "col"))
    tokens_all = row_tile * lax.axis_size("row")
    return (
        updated,
        pair_grad,
        totals[0] / tokens_all,
        totals[1] / tokens_all,
        totals[2] / tokens_all,
        totals[3] / tokens_all,
    )


def solution(mesh):
    return jax.shard_map(
        local,
        mesh=mesh,
        in_specs=(P("row", "col", None), P("row", "col", None), P(), P(), P(), P(), P()),
        out_specs=(P("row", "col", None), P("row", "col", None), P(), P(), P(), P()),
        check_vma=False,
    )
```

profile of v0, /device:TPU:1, one launch (start us, length us, event | category | flops | bytes accessed | tf_op | source)
XLA Modules:
  0.0 564.3 jit_solution(1086619950908574980)
XLA Ops:
  10.0 1.1 fusion.10
  11.9 1.4 fusion.53
  14.3 22.1 %all_to_all.92 = bf16[8,32,16,128]{3,2,1,0:T(8,128)(2,1)S(1)} all-to-all(bf16[8,32,16,128]{3,2,1,0:T(8,128)(2,1)S(1)} %broadcast_in_dim.24), channel_id=1, replica_groups=mesh['row'=8,'col'=16] {'row'}, dimensions={0} | all-to-all | bytes 2097152 | tf_op jit(solution)/shard_map/all_to_all | solution.py:16
  36.4 31.5 %all_to_all.93 = bf16[256,16,128]{2,1,0:T(8,128)(2,1)S(1)} all-to-all(bf16[256,16,128]{2,1,0:T(8,128)(2,1)S(1)} %bitcast.135), channel_id=1, replica_groups=mesh['row'=8,'col'=16] {'col'}, dimensions={0} | all-to-all | bytes 2097152 | tf_op jit(solution)/shard_map/all_to_all | solution.py:64
  67.9 1.3 copy.219
  69.1 2.7 copy.220
  72.3 15.3 %copy.221 = bf16[32,256,128]{0,1,2:T(8,128)(2,1)} copy(bf16[32,256,128]{2,1,0:T(8,128)(2,1)} %all-gather.5.cloned.1.call-done) | data formatting | bytes 4194304 | tf_op jit(solution)/shard_map/all_gather | solution.py:50
  87.6 6.0 %bitcast_reduce_fusion.1 = (f32[32,16]{0,1:T(8,128)S(1)}, f32[128,16,32]{2,1,0:T(8,128)}) fusion(bf16[16,256,128]{1,0,2:T(8,128)(2,1)} %copy.220, bf16[32,256,128]{0,1,2:T(8,128)(2,1)} %copy.221), kind=kOutput, calls=%fused_computation.7 | convolution fusion | flops 33619456 | bytes 3409920 | tf_op jit(solution)/shard_map/ikh,jkh->ijh/dot_general | solution.py:75
  93.6 1.7 copy.222
  101.4 4.2 all-to-all-start.2
  105.7 40.1 %all-gather.7.cloned.1.call-done = bf16[32,256,128]{2,1,0:T(8,128)(2,1)} async-done(((bf16[32,16,128]{2,1,0:T(8,128)(2,1)}), bf16[32,256,128]{2,1,0:T(8,128)(2,1)}) %all-gather.7.cloned.1.call-update) | async-done | bytes 2097168 | tf_op jit(solution)/shard_map/all_gather | solution.py:50
  145.8 4.3 copy.231
  150.1 4.4 all-to-all-start.3
  155.2 3.0 copy.234
  158.2 24.5 %all-to-all-done.3 = bf16[32,256,128]{2,0,1:T(8,128)(2,1)} async-done(((bf16[32,256,128]{2,0,1:T(8,128)(2,1)}), bf16[32,256,128]{2,0,1:T(8,128)(2,1)}, u32[]{:S(2)}, u32[]{:S(2)}) %all-to-all-start.3) | async-done | bytes 2097184 | tf_op jit(solution)/shard_map/all_to_all | solution.py:68
  182.6 3.7 copy.233
  186.4 4.9 copy.235
  191.3 3.6 bitcast_reduce_fusion
  194.8 1.7 copy.236
  196.6 2.0 multiply_reduce_fusion.1
  199.0 1.3 fusion.67
  200.4 1.3 add_convert_fusion.1
  201.9 17.9 %all_to_all.94 = bf16[8,32,16,128]{3,2,1,0:T(8,128)(2,1)} all-to-all(bf16[8,32,16,128]{3,2,1,0:T(8,128)(2,1)S(1)} %broadcast_in_dim.28), channel_id=1, replica_groups=mesh['row'=8,'col'=16] {'row'}, dimensions={0} | all-to-all | bytes 2097152 | tf_op jit(solution)/shard_map/all_to_all | solution.py:16
  219.8 6.1 %all-to-all-start.5 = ((bf16[256,16,128]{2,1,0:T(8,128)(2,1)}), bf16[256,16,128]{2,1,0:T(8,128)(2,1)}, u32[]{:S(2)}, u32[]{:S(2)}) async-start(bf16[256,16,128]{2,1,0:T(8,128)(2,1)} %bitcast.137), calls=%async_computation.5 | async-start | bytes 2097152 | tf_op jit(solution)/shard_map/all_to_all | solution.py:64
  225.9 15.2 %copy.246 = bf16[32,256,128]{0,1,2:T(8,128)(2,1)} copy(bf16[32,256,128]{2,1,0:T(8,128)(2,1)} %all-gather.7.cloned.1.call-done) | data formatting | bytes 4194304 | tf_op jit(solution)/shard_map/all_gather | solution.py:50
  241.2 15.3 %copy.249 = bf16[32,256,128]{0,1,2:T(8,128)(2,1)} copy(bf16[32,256,128]{2,1,0:T(8,128)(2,1)} %all-gather.9.cloned.1.call-done) | data formatting | bytes 4194304 | tf_op jit(solution)/shard_map/all_gather | solution.py:50
  256.5 3.0 copy.245
  259.4 5.9 %fusion.83 = f32[128,16,32]{2,1,0:T(8,128)} fusion(bf16[256,16,128]{0,1,2:T(8,128)(2,1)} %copy.245, bf16[32,256,128]{0,1,2:T(8,128)(2,1)} %copy.246), kind=kOutput, calls=%fused_computation.151 | convolution fusion | flops 33554432 | bytes 3407872 | tf_op jit(solution)/shard_map/kih,ijh->kjh/dot_general | solution.py:105
  265.4 2.3 copy.247
  267.7 2.5 copy.248
  270.2 2.7 copy.250
  272.9 5.9 %fusion.86 = f32[128,32,16]{1,2,0:T(8,128)} fusion(bf16[16,256,128]{1,0,2:T(8,128)(2,1)} %copy.250, bf16[32,256,128]{0,1,2:T(8,128)(2,1)} %copy.249), kind=kOutput, calls=%fused_computation.154 | convolution fusion | flops 33554432 | bytes 3407872 | tf_op jit(solution)/shard_map/ijh,kjh->kih/dot_general | solution.py:102
  278.8 2.4 copy.251
  281.2 2.6 fusion.18
  283.8 1.4 fusion.16
  285.4 1.3 fusion.55
  286.9 2.1 fusion.22
  289.6 2.4 multiply_reduce_fusion
  292.0 1.4 copy.281
  293.4 1.3 multiply_multiply_fusion.1
  294.8 1.4 copy.257
  296.1 1.9 fusion.68
  298.1 1.4 copy.282
  299.5 1.3 negate_multiply_fusion.1
  300.7 1.4 copy.259
  302.1 2.0 add_convert_fusion
  305.2 4.2 all-to-all-start.6
  309.5 42.8 %all-gather.11.cloned.1.call-done = bf16[32,256,128]{2,1,0:T(8,128)(2,1)} async-done(((bf16[32,16,128]{2,1,0:T(8,128)(2,1)}), bf16[32,256,128]{2,1,0:T(8,128)(2,1)}) %all-gather.11.cloned.1.call-update) | async-done | bytes 2097168 | tf_op jit(solution)/shard_map/all_gather | solution.py:50
  352.3 4.3 copy.260
  356.6 4.3 all-to-all-start.7
  361.2 2.1 copy.266
  363.3 3.1 copy.263
  366.4 2.1 convolution_bitcast_fusion.2
  368.6 1.1 convolution_bitcast_fusion.3
  369.8 1.5 convolution_bitcast_fusion
  371.3 15.3 %copy.267 = bf16[32,256,128]{0,1,2:T(8,128)(2,1)} copy(bf16[32,256,128]{2,1,0:T(8,128)(2,1)} %all-gather.11.cloned.1.call-done) | data formatting | bytes 4194304 | tf_op jit(solution)/shard_map/all_gather | solution.py:50
  386.6 4.9 fusion.85
  392.0 3.7 copy.262
  395.7 4.9 copy.264
  400.6 2.6 fusion.84
  404.6 1.5 convolution_bitcast_fusion.1
  408.7 145.6 %all-reduce.13.cloned.1.call-done = (f32[128,640]{1,0:T(8,128)}, f32[128,128]{1,0:T(8,128)}, f32[128,640]{1,0:T(8,128)}, f32[128,128]{1,0:T(8,128)}) async-done(((f32[128,640]{1,0:T(8,128)}, f32[128,128]{1,0:T(8,128)}, f32[128,640]{1,0:T(8,128)}, f32[128,128]{1,0:T(8,128)}), (f32[128,640]{1,0:T(8,128)}, f32[128,128]{1,0:T(8,128)}, f32[128,640]{1,0:T(8,128)}, ...) | async-done | bytes 786448 | tf_op jit(solution)/shard_map/psum | solution.py:173
  554.3 1.5 broadcast_multiply_fusion.2
  555.8 1.9 broadcast_multiply_fusion
  (139 shorter events, 19.5 us)
Async XLA Ops:
  7.2 90.8 %copy-start = (bf16[128,640]{1,0:T(8,128)(2,1)S(1)}, bf16[128,640]{1,0:T(8,128)(2,1)}, u32[]{:S(2)}) copy-start(bf16[128,640]{1,0:T(8,128)(2,1)} %param.12) | copy-start | bytes 491524
  7.2 65.1 %all-gather.5.cloned.1.call-start = ((), (), s32[]{:S(2)}) async-start(), calls=%async_computation.8 | async-start | bytes 2228224 | tf_op jit(solution)/shard_map/all_gather | solution.py:50
  11.2 0.6 copy-start.15
  14.1 131.7 %all-gather.7.cloned.1.call-start = ((), (), s32[]{:S(2)}) async-start(), calls=%async_computation.9 | async-start | bytes 2228224 | tf_op jit(solution)/shard_map/all_gather | solution.py:50
  93.6 2.2 copy-start.2
  93.6 2.2 copy-start.21
  95.7 1.6 copy-start.17
  97.3 0.6 copy-start.18
  98.4 1.1 copy-start.1
  100.3 1.1 copy-start.4
  101.4 48.6 %all-to-all-start.2 = ((bf16[8,32,16,128]{3,2,1,0:T(8,128)(2,1)}), bf16[8,32,16,128]{3,2,1,0:T(8,128)(2,1)}, u32[]{:S(2)}, u32[]{:S(2)}) async-start(bf16[8,32,16,128]{3,2,1,0:T(8,128)(2,1)} %broadcast_in_dim.25), calls=%async_computation.2 | async-start | bytes 2097152 | tf_op jit(solution)/shard_map/all_to_all | solution.py:16
  150.1 32.6 %all-to-all-start.3 = ((bf16[32,256,128]{2,0,1:T(8,128)(2,1)}), bf16[32,256,128]{2,0,1:T(8,128)(2,1)}, u32[]{:S(2)}, u32[]{:S(2)}) async-start(bf16[32,256,128]{2,0,1:T(8,128)(2,1)} %copy.231), calls=%async_computation.3 | async-start | bytes 4194304 | tf_op jit(solution)/shard_map/all_to_all | solution.py:68
  154.4 86.7 %all-gather.9.cloned.1.call-start = ((), (), s32[]{:S(2)}) async-start(), calls=%async_computation.10 | async-start | bytes 2228224 | tf_op jit(solution)/shard_map/all_gather | solution.py:50
  194.8 1.8 copy-start.20
  196.6 84.6 %copy-start.10 = (f32[32,16]{1,0:T(8,128)}, f32[32,16]{1,0:T(8,128)S(1)}, u32[]{:S(2)}) copy-start(f32[32,16]{1,0:T(8,128)S(1)} %copy.238) | copy-start | bytes 6148
  198.9 82.3 %copy-start.12 = (f32[32,16]{1,0:T(8,128)}, f32[32,16]{1,0:T(8,128)S(1)}, u32[]{:S(2)}) copy-start(f32[32,16]{1,0:T(8,128)S(1)} %copy.240) | copy-start | bytes 6148
  219.8 47.9 %all-to-all-start.5 = ((bf16[256,16,128]{2,1,0:T(8,128)(2,1)}), bf16[256,16,128]{2,1,0:T(8,128)(2,1)}, u32[]{:S(2)}, u32[]{:S(2)}) async-start(bf16[256,16,128]{2,1,0:T(8,128)(2,1)} %bitcast.137), calls=%async_computation.5 | async-start | bytes 2097152 | tf_op jit(solution)/shard_map/all_to_all | solution.py:64
  225.9 126.4 %all-gather.11.cloned.1.call-start = ((), (), s32[]{:S(2)}) async-start(), calls=%async_computation.11 | async-start | bytes 2228224 | tf_op jit(solution)/shard_map/all_gather | solution.py:50
  283.7 1.5 copy-start.22
  283.7 1.5 copy-start.24
  283.7 1.5 copy-start.26
  283.8 1.5 copy-start.28
  283.8 1.5 copy-start.30
  283.8 1.5 copy-start.19
  289.0 0.7 copy-start.5
  289.6 14.5 %copy-start.3 = (bf16[32,16,128]{2,1,0:T(8,128)(2,1)S(1)}, bf16[32,16,128]{2,1,0:T(8,128)(2,1)}, u32[]{:S(2)}) copy-start(bf16[32,16,128]{2,1,0:T(8,128)(2,1)} %get-tuple-element.32) | copy-start | bytes 393220
  305.2 51.4 %all-to-all-start.6 = ((bf16[8,32,16,128]{3,2,1,0:T(8,128)(2,1)}), bf16[8,32,16,128]{3,2,1,0:T(8,128)(2,1)}, u32[]{:S(2)}, u32[]{:S(2)}) async-start(bf16[8,32,16,128]{3,2,1,0:T(8,128)(2,1)} %broadcast_in_dim.62), calls=%async_computation.6 | async-start | bytes 2097152 | tf_op jit(solution)/shard_map/all_to_all | solution.py:16
  356.6 35.4 %all-to-all-start.7 = ((bf16[32,256,128]{2,0,1:T(8,128)(2,1)}), bf16[32,256,128]{2,0,1:T(8,128)(2,1)}, u32[]{:S(2)}, u32[]{:S(2)}) async-start(bf16[32,256,128]{2,0,1:T(8,128)(2,1)} %copy.260), calls=%async_computation.7 | async-start | bytes 4194304 | tf_op jit(solution)/shard_map/all_to_all | solution.py:68
  360.9 193.3 %all-reduce.13.cloned.1.call-start = ((), (), s32[]{:S(2)}) async-start(), calls=%async_computation.12 | async-start | bytes 1572864 | tf_op jit(solution)/shard_map/psum | solution.py:173
  363.3 3.1 copy-start.11
  363.3 3.1 copy-start.13
  363.3 3.1 copy-start.14
  366.4 2.1 copy-start.6
  368.5 1.1 copy-start.23
  368.5 1.1 copy-start.25
  368.5 1.1 copy-start.27
  368.5 1.2 copy-start.29
  368.5 1.2 copy-start.31
  403.7 1.0 copy-start.7
  404.6 1.5 copy-start.8
  404.6 1.5 copy-start.9
  406.1 0.9 copy-start.16
Sparse Core Ops, SparseCore 0:
  14.2 58.0 all-gather.4
  100.5 45.2 all-gather.6
  157.6 47.5 all-gather.8
  304.2 48.0 all-gather.10
  407.7 146.5 all-reduce.12
where the time goes:
time: 566 us; the launch traced here: 564 us
  waiting for transfers between devices  254 us (45%)
  local copies, waits for them, and re-layouts  130 us (23%)
  blocking collectives  71.5 us (13%)
  matrix products  47.2 us (8%)
  starting transfers between devices  23.8 us (4%)
  other arithmetic  23.6 us (4%)
  between operations  14.2 us (3%)
    psum x1, waiting for transfers between devices, local(): lax.psum((out_in_part, out_out_part, in_in_part, in_out_part), ('row', 'c...  146 us
    all_gather x4, waiting for transfers between devices, cols_of(): lax.all_gather(shortened(tiles), 'col', axis=1, tiled=True)  83.4 us
    all_gather x6, local copies, waits for them, and re-layouts, cols_of(): lax.all_gather(shortened(tiles), 'col', axis=1, tiled=True)  69.7 us
    all_to_all x2, blocking collectives, from_everyone(): return lax.all_to_all(copies, axis, split_axis=0, concat_axis=0, tiled=True)  40 us
    all_to_all x1, blocking collectives, to_row_blocks(): return lax.all_to_all(panel, 'col', split_axis=0, concat_axis=1, tiled=True)  31.5 us
    all_to_all x2, waiting for transfers between devices, to_col_blocks(): return lax.all_to_all(panel, 'row', split_axis=1, concat_axis=0, tiled=True)  24.5 us
    all_to_all x4, local copies, waits for them, and re-layouts, to_col_blocks(): return lax.all_to_all(panel, 'row', split_axis=1, concat_axis=0, tiled=True)  17.2 us
  transfers between devices with their start and end apart: 10, of which 5 were waited for; matrix products, arithmetic and copies ran while one was open for 20% of the time, Pallas kernels for 0%

commit v1 on v0

--- a/solution.py
+++ b/solution.py
@@ -2,6 +2,7 @@
 import jax.numpy as jnp
 from jax import lax
 from jax.sharding import PartitionSpec as P
+from jax.lax import all_to_all, axis_size
 
 H = 128
 EPSILON = 1e-05
@@ -61,7 +62,17 @@
 
 
 def to_row_blocks(panel):
-    return lax.all_to_all(panel, "col", split_axis=0, concat_axis=1, tiled=True)
+
+    def proceed_the_shapes(page, axis_id):
+        val2 = all_to_all(
+            jnp.stack(jnp.split(page, axis_size(axis_id), axis=0), axis=0),
+            axis_name=axis_id,
+            concat_axis=0,
+            split_axis=0,
+        )
+        return jnp.concatenate(val2, axis=1)
+
+    return proceed_the_shapes(panel, "col")
 
 
 def to_col_blocks(panel):

time: 566 us -> 619 us (1.094); the launches traced: 564 us -> 610 us
  blocking collectives: 71.5 us -> 26.2 us
  waiting for transfers between devices: 254 us -> 297 us
  local copies, waits for them, and re-layouts: 130 us -> 155 us
  starting transfers between devices: 23.8 us -> 45.9 us
    all_to_all x3 -> x1, blocking collectives: 71.5 us -> 26.2 us  [proceed_the_shapes(): all_to_all(jnp.stack(jnp.split(page, axis_size(axis_id), axis=0), axis=0)...]
    all_to_all x2 -> x4, waiting for transfers between devices: 0.01 us -> 27.4 us  [from_everyone(): return lax.all_to_all(copies, axis, split_axis=0, concat_axis=0, tiled=True)]
    unnamed x70 -> x100, local copies, waits for them, and re-layouts: 6.82 us -> 28.9 us
    all_gather x4, waiting for transfers between devices: 83.4 us -> 99.4 us  [cols_of(): lax.all_gather(shortened(tiles), 'col', axis=1, tiled=True)]
    all_to_all x2, starting transfers between devices: 8.7 us -> 20.5 us  [to_col_blocks(): return lax.all_to_all(panel, 'row', split_axis=1, concat_axis=0, tiled=True)]
    all_to_all x2 -> x4, starting transfers between devices: 8.48 us -> 18.7 us  [from_everyone(): return lax.all_to_all(copies, axis, split_axis=0, concat_axis=0, tiled=True)]
    all_to_all x4 -> x0, local copies, waits for them, and re-layouts: 9.12 us -> none  [to_row_blocks(): return lax.all_to_all(panel, 'col', split_axis=0, concat_axis=1, tiled=True)]
    reshape x0 -> x4, local copies, waits for them, and re-layouts: none -> 9.1 us  [proceed_the_shapes(): return jnp.concatenate(val2, axis=1)]
  transfers between devices with their start and end apart: 10 -> 12, of which waited for: 5 -> 7; matrix products, arithmetic and copies ran while one was open for 20% -> 19% of each run, Pallas kernels for 0% -> 0%
where the time goes in v1:
time: 619 us; the launch traced here: 610 us
  waiting for transfers between devices  297 us (48%)
  local copies, waits for them, and re-layouts  155 us (25%)
  matrix products  47.2 us (8%)
  starting transfers between devices  45.9 us (7%)
  blocking collectives  26.2 us (4%)
  other arithmetic  23.7 us (4%)
  between operations  14.6 us (2%)
    psum x1, waiting for transfers between devices, local(): lax.psum((out_in_part, out_out_part, in_in_part, in_out_part), ('row', 'c...  146 us
    all_gather x4, waiting for transfers between devices, cols_of(): lax.all_gather(shortened(tiles), 'col', axis=1, tiled=True)  99.4 us
    all_gather x6, local copies, waits for them, and re-layouts, cols_of(): lax.all_gather(shortened(tiles), 'col', axis=1, tiled=True)  69.6 us
    unnamed x100, local copies, waits for them, and re-layouts  28.9 us
    all_to_all x4, waiting for transfers between devices, from_everyone(): return lax.all_to_all(copies, axis, split_axis=0, concat_axis=0, tiled=True)  27.4 us
    all_to_all x1, blocking collectives, proceed_the_shapes(): all_to_all(jnp.stack(jnp.split(page, axis_size(axis_id), axis=0), axis=0)...  26.2 us
    all_to_all x2, waiting for transfers between devices, to_col_blocks(): return lax.all_to_all(panel, 'row', split_axis=1, concat_axis=0, tiled=True)  23.6 us
    all_to_all x2, starting transfers between devices, to_col_blocks(): return lax.all_to_all(panel, 'row', split_axis=1, concat_axis=0, tiled=True)  20.5 us
  transfers between devices with their start and end apart: 12, of which 7 were waited for; matrix products, arithmetic and copies ran while one was open for 19% of the time, Pallas kernels for 0%

profile of v1, /device:TPU:1, one launch (start us, length us, event | category | flops | bytes accessed | tf_op | source)
XLA Modules:
  0.0 610.4 jit_solution(8245358000467417501)
XLA Ops:
  15.2 5.9 all-to-all-start
  21.9 13.8 %all-to-all-done = bf16[8,32,16,128]{3,2,1,0:T(8,128)(2,1)S(1)} async-done(((bf16[8,32,16,128]{3,2,1,0:T(8,128)(2,1)}), bf16[8,32,16,128]{3,2,1,0:T(8,128)(2,1)S(1)}, u32[]{:S(2)}, u32[]{:S(2)}) %all-to-all-start) | async-done | bytes 1048608 | tf_op jit(solution)/shard_map/all_to_all | solution.py:17
  36.0 26.2 %all_to_all.66 = bf16[16,16,16,128]{3,2,1,0:T(8,128)(2,1)S(1)} all-to-all(bf16[16,16,16,128]{3,2,1,0:T(8,128)(2,1)S(1)} %constant_dynamic-update-slice_fusion), channel_id=1, replica_groups=mesh['row'=8,'col'=16] {'col'}, dimensions={0} | all-to-all | bytes 2097152 | tf_op jit(solution)/shard_map/all_to_all | solution.py:67
  63.4 2.7 copy.219
  66.1 15.1 %all-gather.5.cloned.1.call-done = bf16[32,256,128]{2,1,0:T(8,128)(2,1)} async-done(((bf16[32,16,128]{2,1,0:T(8,128)(2,1)}), bf16[32,256,128]{2,1,0:T(8,128)(2,1)}) %all-gather.5.cloned.1.call-update) | async-done | bytes 2097168 | tf_op jit(solution)/shard_map/all_gather | solution.py:51
  81.2 15.3 %copy.220 = bf16[32,256,128]{0,1,2:T(8,128)(2,1)} copy(bf16[32,256,128]{2,1,0:T(8,128)(2,1)} %all-gather.5.cloned.1.call-done) | data formatting | bytes 4194304 | tf_op jit(solution)/shard_map/all_gather | solution.py:51
  96.5 6.0 bitcast_reduce_fusion.1
  102.5 1.7 copy.221
  110.4 4.2 all-to-all-start.2
  114.7 41.3 %all-gather.7.cloned.1.call-done = bf16[32,256,128]{2,1,0:T(8,128)(2,1)} async-done(((bf16[32,16,128]{2,1,0:T(8,128)(2,1)}), bf16[32,256,128]{2,1,0:T(8,128)(2,1)}) %all-gather.7.cloned.1.call-update) | async-done | bytes 2097168 | tf_op jit(solution)/shard_map/all_gather | solution.py:51
  156.0 4.3 copy.230
  160.3 16.1 %all-to-all-start.3 = ((bf16[32,256,128]{2,0,1:T(8,128)(2,1)}), bf16[32,256,128]{2,0,1:T(8,128)(2,1)}, u32[]{:S(2)}, u32[]{:S(2)}) async-start(bf16[32,256,128]{2,0,1:T(8,128)(2,1)} %copy.230), calls=%async_computation.3 | async-start | bytes 4194304 | tf_op jit(solution)/shard_map/all_to_all | solution.py:79
  176.4 3.0 copy.233
  179.4 23.6 %all-to-all-done.3 = bf16[32,256,128]{2,0,1:T(8,128)(2,1)} async-done(((bf16[32,256,128]{2,0,1:T(8,128)(2,1)}), bf16[32,256,128]{2,0,1:T(8,128)(2,1)}, u32[]{:S(2)}, u32[]{:S(2)}) %all-to-all-start.3) | async-done | bytes 2097184 | tf_op jit(solution)/shard_map/all_to_all | solution.py:79
  203.0 3.8 copy.232
  206.7 4.9 copy.234
  211.6 3.6 bitcast_reduce_fusion
  215.2 1.7 copy.235
  217.0 2.0 multiply_reduce_fusion.1
  223.2 4.2 all-to-all-start.4
  228.2 13.6 %all-to-all-done.4 = bf16[8,32,16,128]{3,2,1,0:T(8,128)(2,1)} async-done(((bf16[8,32,16,128]{3,2,1,0:T(8,128)(2,1)}), bf16[8,32,16,128]{3,2,1,0:T(8,128)(2,1)}, u32[]{:S(2)}, u32[]{:S(2)}) %all-to-all-start.4) | async-done | bytes 1048608 | tf_op jit(solution)/shard_map/all_to_all | solution.py:17
  241.9 1.5 constant_dynamic-update-slice_fusion.31
  243.3 1.5 constant_dynamic-update-slice_fusion.30
  244.8 1.5 constant_dynamic-update-slice_fusion.29
  246.2 1.5 constant_dynamic-update-slice_fusion.28
  249.2 1.5 constant_dynamic-update-slice_fusion.26
  253.5 1.5 constant_dynamic-update-slice_fusion.23
  255.0 1.5 constant_dynamic-update-slice_fusion.22
  256.5 1.5 constant_dynamic-update-slice_fusion.21
  259.4 1.5 constant_dynamic-update-slice_fusion.19
  260.8 1.5 constant_dynamic-update-slice_fusion.18
  262.3 1.5 constant_dynamic-update-slice_fusion.17
  265.2 6.4 %all-to-all-start.5 = ((bf16[16,16,16,128]{3,2,1,0:T(8,128)(2,1)}), bf16[16,16,16,128]{3,2,1,0:T(8,128)(2,1)}, u32[]{:S(2)}, u32[]{:S(2)}) async-start(bf16[16,16,16,128]{3,2,1,0:T(8,128)(2,1)} %constant_dynamic-update-slice_fusion.16), calls=%async_computation.5 | async-start | bytes 2097152 | tf_op jit(solution)/shard_map/all_to_all | solution.py:67
  271.6 15.2 %copy.245 = bf16[32,256,128]{0,1,2:T(8,128)(2,1)} copy(bf16[32,256,128]{2,1,0:T(8,128)(2,1)} %all-gather.7.cloned.1.call-done) | data formatting | bytes 4194304 | tf_op jit(solution)/shard_map/all_gather | solution.py:51
  286.9 15.3 %copy.248 = bf16[32,256,128]{0,1,2:T(8,128)(2,1)} copy(bf16[32,256,128]{2,1,0:T(8,128)(2,1)} %all-gather.9.cloned.1.call-done) | data formatting | bytes 4194304 | tf_op jit(solution)/shard_map/all_gather | solution.py:51
  302.2 3.0 copy.244
  305.2 5.9 fusion.83
  311.0 2.4 copy.246
  313.4 2.5 copy.247
  315.9 2.7 copy.249
  318.6 5.9 fusion.86
  324.5 2.4 copy.250
  326.9 2.6 fusion.18
  332.6 2.1 fusion.22
  335.3 2.4 multiply_reduce_fusion
  341.8 1.9 fusion.68
  347.8 2.0 add_convert_fusion
  350.9 4.2 all-to-all-start.6
  355.2 42.9 %all-gather.11.cloned.1.call-done = bf16[32,256,128]{2,1,0:T(8,128)(2,1)} async-done(((bf16[32,16,128]{2,1,0:T(8,128)(2,1)}), bf16[32,256,128]{2,1,0:T(8,128)(2,1)}) %all-gather.11.cloned.1.call-update) | async-done | bytes 2097168 | tf_op jit(solution)/shard_map/all_gather | solution.py:51
  398.0 4.2 copy.259
  402.3 4.4 all-to-all-start.7
  406.9 2.1 copy.265
  409.0 3.1 copy.262
  412.1 2.1 convolution_bitcast_fusion.2
  415.4 1.5 convolution_bitcast_fusion
  416.9 15.3 %copy.266 = bf16[32,256,128]{0,1,2:T(8,128)(2,1)} copy(bf16[32,256,128]{2,1,0:T(8,128)(2,1)} %all-gather.11.cloned.1.call-done) | data formatting | bytes 4194304 | tf_op jit(solution)/shard_map/all_gather | solution.py:51
  432.2 4.9 fusion.85
  437.6 3.7 copy.261
  441.4 4.9 copy.263
  446.3 2.6 fusion.84
  450.3 1.5 convolution_bitcast_fusion.1
  454.3 145.7 %all-reduce.13.cloned.1.call-done = (f32[128,640]{1,0:T(8,128)}, f32[128,128]{1,0:T(8,128)}, f32[128,640]{1,0:T(8,128)}, f32[128,128]{1,0:T(8,128)}) async-done(((f32[128,640]{1,0:T(8,128)}, f32[128,128]{1,0:T(8,128)}, f32[128,640]{1,0:T(8,128)}, f32[128,128]{1,0:T(8,128)}), (f32[128,640]{1,0:T(8,128)}, f32[128,128]{1,0:T(8,128)}, f32[128,640]{1,0:T(8,128)}, ...) | async-done | bytes 786448 | tf_op jit(solution)/shard_map/psum | solution.py:184
  600.0 1.5 broadcast_multiply_fusion.2
  601.5 1.9 broadcast_multiply_fusion
  (173 shorter events, 47.5 us)
Async XLA Ops:
  7.2 99.8 %copy-start = (bf16[128,640]{1,0:T(8,128)(2,1)S(1)}, bf16[128,640]{1,0:T(8,128)(2,1)}, u32[]{:S(2)}) copy-start(bf16[128,640]{1,0:T(8,128)(2,1)} %param.12) | copy-start | bytes 491524
  11.2 0.6 copy-start.15
  15.2 20.5 %all-to-all-start = ((bf16[8,32,16,128]{3,2,1,0:T(8,128)(2,1)}), bf16[8,32,16,128]{3,2,1,0:T(8,128)(2,1)S(1)}, u32[]{:S(2)}, u32[]{:S(2)}) async-start(bf16[8,32,16,128]{3,2,1,0:T(8,128)(2,1)} %broadcast_in_dim.24), calls=%async_computation | async-start | bytes 2097152 | tf_op jit(solution)/shard_map/all_to_all | solution.py:17
  21.1 60.1 %all-gather.5.cloned.1.call-start = ((), (), s32[]{:S(2)}) async-start(), calls=%async_computation.8 | async-start | bytes 2228224 | tf_op jit(solution)/shard_map/all_gather | solution.py:51
  21.9 134.1 %all-gather.7.cloned.1.call-start = ((), (), s32[]{:S(2)}) async-start(), calls=%async_computation.9 | async-start | bytes 2228224 | tf_op jit(solution)/shard_map/all_gather | solution.py:51
  102.5 2.2 copy-start.2
  102.5 2.2 copy-start.21
  104.6 1.6 copy-start.17
  106.2 0.6 copy-start.18
  107.3 1.1 copy-start.1
  109.3 1.1 copy-start.4
  110.4 49.9 %all-to-all-start.2 = ((bf16[8,32,16,128]{3,2,1,0:T(8,128)(2,1)}), bf16[8,32,16,128]{3,2,1,0:T(8,128)(2,1)}, u32[]{:S(2)}, u32[]{:S(2)}) async-start(bf16[8,32,16,128]{3,2,1,0:T(8,128)(2,1)} %broadcast_in_dim.25), calls=%async_computation.2 | async-start | bytes 2097152 | tf_op jit(solution)/shard_map/all_to_all | solution.py:17
  160.3 42.7 %all-to-all-start.3 = ((bf16[32,256,128]{2,0,1:T(8,128)(2,1)}), bf16[32,256,128]{2,0,1:T(8,128)(2,1)}, u32[]{:S(2)}, u32[]{:S(2)}) async-start(bf16[32,256,128]{2,0,1:T(8,128)(2,1)} %copy.230), calls=%async_computation.3 | async-start | bytes 4194304 | tf_op jit(solution)/shard_map/all_to_all | solution.py:79
  215.2 1.8 copy-start.20
  217.0 109.9 %copy-start.10 = (f32[32,16]{1,0:T(8,128)}, f32[32,16]{1,0:T(8,128)S(1)}, u32[]{:S(2)}) copy-start(f32[32,16]{1,0:T(8,128)S(1)} %copy.237) | copy-start | bytes 6148
  219.3 107.6 %copy-start.12 = (f32[32,16]{1,0:T(8,128)}, f32[32,16]{1,0:T(8,128)S(1)}, u32[]{:S(2)}) copy-start(f32[32,16]{1,0:T(8,128)S(1)} %copy.239) | copy-start | bytes 6148
  223.2 18.6 %all-to-all-start.4 = ((bf16[8,32,16,128]{3,2,1,0:T(8,128)(2,1)}), bf16[8,32,16,128]{3,2,1,0:T(8,128)(2,1)}, u32[]{:S(2)}, u32[]{:S(2)}) async-start(bf16[8,32,16,128]{3,2,1,0:T(8,128)(2,1)} %broadcast_in_dim.28), calls=%async_computation.4 | async-start | bytes 2097152 | tf_op jit(solution)/shard_map/all_to_all | solution.py:17
  227.5 59.4 %all-gather.9.cloned.1.call-start = ((), (), s32[]{:S(2)}) async-start(), calls=%async_computation.10 | async-start | bytes 2228224 | tf_op jit(solution)/shard_map/all_gather | solution.py:51
  265.2 48.2 %all-to-all-start.5 = ((bf16[16,16,16,128]{3,2,1,0:T(8,128)(2,1)}), bf16[16,16,16,128]{3,2,1,0:T(8,128)(2,1)}, u32[]{:S(2)}, u32[]{:S(2)}) async-start(bf16[16,16,16,128]{3,2,1,0:T(8,128)(2,1)} %constant_dynamic-update-slice_fusion.16), calls=%async_computation.5 | async-start | bytes 2097152 | tf_op jit(solution)/shard_map/all_to_all | solution.py:67
  271.6 126.4 %all-gather.11.cloned.1.call-start = ((), (), s32[]{:S(2)}) async-start(), calls=%async_computation.11 | async-start | bytes 2228224 | tf_op jit(solution)/shard_map/all_gather | solution.py:51
  329.4 1.5 copy-start.22
  329.4 1.5 copy-start.24
  329.4 1.5 copy-start.26
  329.4 1.5 copy-start.28
  329.4 1.5 copy-start.30
  329.5 1.5 copy-start.19
  334.7 0.7 copy-start.5
  335.3 14.5 %copy-start.3 = (bf16[32,16,128]{2,1,0:T(8,128)(2,1)S(1)}, bf16[32,16,128]{2,1,0:T(8,128)(2,1)}, u32[]{:S(2)}) copy-start(bf16[32,16,128]{2,1,0:T(8,128)(2,1)} %get-tuple-element.32) | copy-start | bytes 393220
  350.9 51.4 %all-to-all-start.6 = ((bf16[8,32,16,128]{3,2,1,0:T(8,128)(2,1)}), bf16[8,32,16,128]{3,2,1,0:T(8,128)(2,1)}, u32[]{:S(2)}, u32[]{:S(2)}) async-start(bf16[8,32,16,128]{3,2,1,0:T(8,128)(2,1)} %broadcast_in_dim.62), calls=%async_computation.6 | async-start | bytes 2097152 | tf_op jit(solution)/shard_map/all_to_all | solution.py:17
  402.3 35.3 %all-to-all-start.7 = ((bf16[32,256,128]{2,0,1:T(8,128)(2,1)}), bf16[32,256,128]{2,0,1:T(8,128)(2,1)}, u32[]{:S(2)}, u32[]{:S(2)}) async-start(bf16[32,256,128]{2,0,1:T(8,128)(2,1)} %copy.259), calls=%async_computation.7 | async-start | bytes 4194304 | tf_op jit(solution)/shard_map/all_to_all | solution.py:79
  406.7 193.3 %all-reduce.13.cloned.1.call-start = ((), (), s32[]{:S(2)}) async-start(), calls=%async_computation.12 | async-start | bytes 1572864 | tf_op jit(solution)/shard_map/psum | solution.py:184
  409.0 3.1 copy-start.11
  409.0 3.1 copy-start.13
  409.0 3.1 copy-start.14
  412.1 2.1 copy-start.6
  414.2 1.1 copy-start.23
  414.2 1.1 copy-start.25
  414.2 1.1 copy-start.27
  414.2 1.2 copy-start.29
  414.2 1.2 copy-start.31
  449.3 1.0 copy-start.7
  450.3 1.5 copy-start.8
  450.3 1.5 copy-start.9
  451.8 0.9 copy-start.16
Sparse Core Ops, SparseCore 0:
  24.8 56.3 all-gather.4
  109.4 46.5 all-gather.6
  230.7 46.6 all-gather.8
  349.9 48.0 all-gather.10
  453.4 146.5 all-reduce.12
